TPU v7x, 256 devices: a whole 4x4x8 slice. The times are simulated.
256 devices in a mesh: tile: 64 (over z, x, core), mp: 4 (over y).
Axes of the slice: x: 4, y: 4, z: 8, core: 2. Of those that a mesh axis runs over, the one named last changes fastest.
Arguments:
- latent: bfloat16 [768, 384], P('tile'), may hold values from -19 to 19, as said below
- reward_grad: float32 [768, 384], P('tile'), may hold values from -6 to 6
- curvature: float32 [768, 384], P('tile'), may hold values from 0.3 to 3
- offsets: int32 [128, 2], P('tile'), may hold values from 0 to 736, as said below
- counts: int32 [768, 96], P('tile'), may hold values from 1 to 4, as said below
- w_in: bfloat16 [16, 640], replicated, may hold values from -3.2 to 3.2, as said below
- w_value: bfloat16 [640, 2560], P(None, 'mp'), may hold values from -0.25 to 0.25
- w_gate: bfloat16 [640, 2560], P(None, 'mp'), may hold values from -0.25 to 0.25
- w_down: bfloat16 [2560, 640], P('mp'), may hold values from -0.125 to 0.125
- w_out: bfloat16 [640, 16], replicated, may hold values from -0.25 to 0.25
Outputs:
- blended: float32 [768, 384], P('tile')
- grad_in: float32 [16, 640], replicated
- grad_value: float32 [640, 2560], P(None, 'mp')
- grad_gate: float32 [640, 2560], P(None, 'mp')
- grad_down: float32 [2560, 640], P('mp')
- grad_out: float32 [640, 16], replicated
Inputs may be any that keep to these rules, and one draw needn't show every extreme that they name: `offsets`: the corners are the points of a grid of 32 by 4 points spaced 24, each point taken by exactly one tile in a random order, each moved by at most 4 along each direction; the grid's first row and column stay at 0 and its last row and column are clamped to 736 and 64. The tiles cover every cell of the canvas. `counts`: the number of tiles whose 32 x 32 square holds the cell. `latent`: Real-valued. `w_in`: Real-valued.
All inputs are finite; a program needn't handle non-finite values.
Results may differ from a plain program's by a relative error of at most 0.003.
The roundings to bfloat16 on the way count: a program that leaves them out, or rounds other values in their place, can miss the bound.
Values may be sent and summed in bfloat16 or wider, within the bound.
A program may use at most 64 MiB of HBM per device.

v0:
```python
import math
import jax
import jax.numpy as jnp
from jax import lax
from jax.sharding import PartitionSpec as P

S = 32
layer_eps = 1e-05
root_half = 0.7071067811865476
inv_root_two_pi = 0.3989422804014327
highest = lax.Precision.HIGHEST


def gelu_value(inputs):
    return 0.5 * inputs * (1.0 + lax.erf(inputs * root_half))


def gelu_slope(inputs):
    return (
        0.5 * (1.0 + lax.erf(inputs * root_half))
        + inputs * jnp.exp(-0.5 * inputs * inputs) * inv_root_two_pi
    )


def patchify(cropped, channels):
    half_side = cropped.shape[0] // 2
    return (
        cropped.reshape(half_side, 2, half_side, 2 * channels)
        .transpose(0, 2, 1, 3)
        .reshape(half_side * half_side, 4 * channels)
    )


def unpatch(tokens, tile_side, channels):
    half_side = tile_side // 2
    token_rows = tokens.shape[0] // half_side
    return (
        tokens.reshape(token_rows, half_side, 2, 2 * channels)
        .transpose(0, 2, 1, 3)
        .reshape(2 * token_rows, tile_side * channels)
    )


def layer_norm(hidden):
    values = hidden.astype(jnp.float32)
    center = values - jnp.mean(values, axis=-1, keepdims=True)
    variance = jnp.mean(center * center, axis=-1, keepdims=True)
    inv_scale = lax.rsqrt(variance + layer_eps)
    return (center * inv_scale, inv_scale)


def norm_backward(normed, inv_scale, d_unit):
    centered = d_unit - jnp.mean(d_unit, axis=-1, keepdims=True)
    return inv_scale * (centered - normed * jnp.mean(d_unit * normed, axis=-1, keepdims=True))


def contract_rows(left, right):
    return lax.dot_general(
        left, right, (((0,), (0,)), ((), ())), preferred_element_type=jnp.float32
    )


def contract_rows_exact(left, right):
    return lax.dot_general(
        left, right, (((0,), (0,)), ((), ())), precision=highest, preferred_element_type=jnp.float32
    )


def contract_cols(left, right):
    return lax.dot_general(
        left, right, (((1,), (1,)), ((), ())), preferred_element_type=jnp.float32
    )


def crop_tiles(source, corners, tile_side, channels):

    def crop_one(corner):
        cropped = lax.dynamic_slice(
            source, (corner[0], corner[1] * channels), (tile_side, tile_side * channels)
        )
        return patchify(cropped, channels)

    return jax.vmap(crop_one)(corners)


def place_tiles(canvas, pieces, corners, row_shift, channels):
    piece_rows = pieces.shape[1]
    piece_cols = pieces.shape[2]

    def add_tile(tile_index, current):
        corner = corners[tile_index]
        start_row = corner[0] + row_shift
        start_col = corner[1] * channels
        existing = lax.dynamic_slice(current, (start_row, start_col), (piece_rows, piece_cols))
        return lax.dynamic_update_slice(
            current, existing + pieces[tile_index], (start_row, start_col)
        )

    return lax.fori_loop(0, pieces.shape[0], add_tile, canvas)


def per_device(
    latent, reward_grad, curvature, offsets, counts, w_in, w_value, w_gate, w_down, w_out
):
    channels = w_in.shape[0] // 4
    model_width = w_in.shape[1]
    tile_side = S
    half_side = tile_side // 2
    token_count = half_side * half_side
    tiles_here = offsets.shape[0]
    slab_rows = latent.shape[0]
    canvas_cols = latent.shape[1]
    tile_devices = lax.axis_size("tile")
    model_devices = lax.axis_size("mp")
    model_pos = lax.axis_index("mp")
    share_tokens = token_count // model_devices
    share_pixels = tile_side // model_devices
    scale_factor = 16.0 / math.sqrt(tiles_here * tile_devices * token_count)
    w_out_wide = w_out.astype(jnp.float32)
    cover_count = jnp.repeat(counts, channels, axis=1).astype(jnp.float32)
    placed_row = model_pos * share_pixels
    latent_source = lax.all_gather(latent, "tile", axis=0, tiled=True)
    patches = crop_tiles(latent_source, offsets, tile_side, channels)
    flat_patches = jnp.transpose(patches, (1, 0, 2)).reshape(token_count * tiles_here, 4 * channels)
    hidden = jnp.dot(flat_patches, w_in, preferred_element_type=jnp.float32).astype(jnp.bfloat16)
    normed, inv_scale = layer_norm(hidden)
    unit_in = normed.astype(jnp.bfloat16)
    value_proj = jnp.dot(unit_in, w_value, preferred_element_type=jnp.float32)
    gate_proj = jnp.dot(unit_in, w_gate, preferred_element_type=jnp.float32)
    active = (value_proj * gelu_value(gate_proj)).astype(jnp.bfloat16)
    active_grid = active.reshape(token_count, tiles_here, active.shape[1])

    def take_share(values):
        grid = values.reshape(token_count, tiles_here, values.shape[-1])
        picked = lax.dynamic_slice_in_dim(grid, model_pos * share_tokens, share_tokens, 0)
        return picked.reshape(share_tokens * tiles_here, values.shape[-1])

    hidden_share = take_share(hidden)
    row_block = active_grid.reshape(
        lax.axis_size("mp") * share_tokens * tiles_here, active_grid.shape[2]
    )
    ff_share = lax.psum_scatter(
        jnp.dot(row_block, w_down, preferred_element_type=jnp.float32).reshape(
            lax.axis_size("mp") * share_tokens, tiles_here, model_width
        ),
        "mp",
        scatter_dimension=0,
        tiled=True,
    ).reshape(share_tokens * tiles_here, model_width)
    noise_share = jnp.dot(hidden_share, w_out, preferred_element_type=jnp.float32) + jnp.dot(
        ff_share, w_out_wide, precision=highest, preferred_element_type=jnp.float32
    )
    noise_tiles = jnp.transpose(
        noise_share.reshape(share_tokens, tiles_here, w_out.shape[1]), (1, 0, 2)
    )

    def unpatch_share(tokens):
        return unpatch(tokens, tile_side, channels)

    noise_pieces = jax.vmap(unpatch_share)(noise_tiles)
    canvas_term = place_tiles(
        jnp.zeros((slab_rows * tile_devices, canvas_cols), jnp.float32),
        noise_pieces,
        offsets,
        placed_row,
        channels,
    )
    share_total = lax.psum_scatter(canvas_term, ("tile", "mp"), scatter_dimension=0, tiled=True)
    rows_each = slab_rows // model_devices
    first_share = model_pos * rows_each
    share_cover = lax.dynamic_slice_in_dim(cover_count, first_share, rows_each, 0)
    share_reward = lax.dynamic_slice_in_dim(reward_grad, first_share, rows_each, 0)
    share_curve = lax.dynamic_slice_in_dim(curvature, first_share, rows_each, 0)
    share_blend = share_total / share_cover
    share_cot = ((share_reward - share_curve * share_blend) / share_cover * scale_factor).astype(
        jnp.bfloat16
    )
    blended = lax.all_gather(share_blend, "mp", axis=0, tiled=True)
    cot_source = lax.all_gather(share_cot, ("tile", "mp"), axis=0, tiled=True)
    cot_patches = crop_tiles(cot_source, offsets, tile_side, channels)
    cot_flat = jnp.transpose(cot_patches, (1, 0, 2)).reshape(token_count * tiles_here, 4 * channels)
    cot_share = take_share(cot_flat)
    d_feat = contract_cols(cot_flat, w_out)
    d_feat_b = d_feat.astype(jnp.bfloat16)
    d_active = contract_cols(d_feat_b, w_down)
    down_term = contract_rows(active, d_feat_b)
    d_value = (d_active * gelu_value(gate_proj)).astype(jnp.bfloat16)
    d_gate = (d_active * value_proj * gelu_slope(gate_proj)).astype(jnp.bfloat16)
    value_term = contract_rows(unit_in, d_value)
    gate_term = contract_rows(unit_in, d_gate)
    d_value_grid = d_value.reshape(token_count, tiles_here, d_value.shape[1])
    d_gate_grid = d_gate.reshape(token_count, tiles_here, d_gate.shape[1])
    value_block = d_value_grid.reshape(
        share_tokens * lax.axis_size("mp") * tiles_here, d_value.shape[1]
    )
    gate_block = d_gate_grid.reshape(
        share_tokens * lax.axis_size("mp") * tiles_here, d_gate.shape[1]
    )
    summed = contract_cols(value_block, w_value) + contract_cols(gate_block, w_gate)
    d_unit_share = (
        lax.psum_scatter(
            summed.reshape(share_tokens * lax.axis_size("mp"), tiles_here, model_width).astype(
                jnp.bfloat16
            ),
            "mp",
            scatter_dimension=0,
            tiled=True,
        )
        .astype(jnp.float32)
        .reshape(share_tokens * tiles_here, model_width)
    )
    d_hidden = (
        take_share(d_feat) + norm_backward(take_share(normed), take_share(inv_scale), d_unit_share)
    ).astype(jnp.bfloat16)
    in_term = contract_rows(take_share(flat_patches), d_hidden)
    out_term = contract_rows(hidden_share, cot_share) + contract_rows_exact(
        ff_share, cot_share.astype(jnp.float32)
    )
    grad_in, grad_out = lax.psum((in_term, out_term), ("tile", "mp"))
    grad_value, grad_gate, grad_down = lax.psum((value_term, gate_term, down_term), "tile")
    return (blended, grad_in, grad_value, grad_gate, grad_down, grad_out)


def solution(mesh):
    return jax.shard_map(
        per_device,
        mesh=mesh,
        in_specs=(
            P("tile", None),
            P("tile", None),
            P("tile", None),
            P("tile", None),
            P("tile", None),
            P(),
            P(None, "mp"),
            P(None, "mp"),
            P("mp", None),
            P(),
        ),
        out_specs=(P("tile", None), P(), P(None, "mp"), P(None, "mp"), P("mp", None), P()),
        check_vma=False,
    )
```

profile of v0, /device:TPU:97, one launch (start us, length us, event | category | flops | bytes accessed | tf_op | source)
XLA Modules:
  0.0 971.2 jit_solution(10086862064302789510)
XLA Ops:
  8.1 51.5 %all-gather = bf16[64,12,384]{2,1,0:T(8,128)(2,1)S(1)} all-gather(bf16[1,12,384]{2,1,0:T(8,128)(2,1)} %bitcast.107), channel_id=1, replica_groups=mesh['tile'=64,'mp'=4] {'tile'}, dimensions={0}, use_global_device_ids=true | all-gather | bytes 599040 | tf_op jit(solution)/shard_map/all_gather | solution.py:122
  59.8 4.0 while.16
  60.4 1.4 bitcast_dynamic-update-slice_fusion.4
  66.5 1.9 multiply_convert_fusion.1
  69.2 1.8 reshape.143
  73.2 48.7 %all-reduce.9.cloned.1.call-done = f32[256,2,640]{2,1,0:T(2,128)} async-done(((f32[256,2,640]{2,1,0:T(2,128)}), f32[256,2,640]{2,1,0:T(2,128)}) %all-reduce.9.cloned.1.call-update) | async-done | bytes 1310736
  124.1 5.1 while.15
  133.9 259.7 %all-reduce.11.cloned.1.call-done = f32[768,384]{0,1:T(8,128)} async-done(((f32[768,384]{0,1:T(8,128)}), f32[768,384]{0,1:T(8,128)}) %all-reduce.11.cloned.1.call-update) | async-done | bytes 1179664
  393.6 1.9 fusion.23
  395.6 70.2 %all-gather.2 = bf16[256,3,384]{2,1,0:T(4,128)(2,1)S(1)} all-gather(bf16[1,3,384]{2,1,0:T(4,128)(2,1)S(1)} %copy.75), channel_id=1, replica_groups=mesh['tile'=64,'mp'=4] {'tile','mp'}, dimensions={0}, use_global_device_ids=true | all-gather | bytes 592128 | tf_op jit(solution)/shard_map/all_gather | solution.py:179
  466.3 4.0 while.17
  466.9 1.4 bitcast_dynamic-update-slice_fusion.5
  468.9 1.4 bitcast_dynamic-update-slice_fusion.5
  473.0 2.9 fusion.9
  477.5 1.6 fusion.2
  479.1 2.6 convert_element_type.57
  481.7 2.0 copy.80
  484.7 2.9 reshape.152
  487.6 1.7 constant_dynamic-slice_fusion.3
  489.4 1.8 reshape.151
  491.2 1.7 constant_dynamic-slice_fusion.5
  494.2 1.8 fusion.10
  496.0 3.1 fusion.35
  499.2 1.9 fusion.17
  501.0 4.6 reduce-scatter.3.cloned.1.call-done
  506.8 2.1 convolution_bitcast_fusion.2
  509.0 2.0 fusion.37
  512.0 9.1 all-gather.1
  521.7 235.5 %all-reduce.13.cloned.1.call-done = (f32[16,640]{1,0:T(8,128)}, f32[640,16]{0,1:T(8,128)}) async-done(((f32[16,640]{1,0:T(8,128)}, f32[640,16]{0,1:T(8,128)}), (f32[16,640]{1,0:T(8,128)}, f32[640,16]{0,1:T(8,128)})) %all-reduce.13.cloned.1.call-update) | async-done | bytes 81936 | tf_op jit(solution)/shard_map/psum | solution.py:219
  757.3 199.4 %all-reduce.15.cloned.1.call-done = (f32[640,640]{1,0:T(8,128)}, f32[640,640]{1,0:T(8,128)}, f32[640,640]{1,0:T(8,128)}) async-done(((f32[640,640]{1,0:T(8,128)}, f32[640,640]{1,0:T(8,128)}, f32[640,640]{1,0:T(8,128)}), (f32[640,640]{1,0:T(8,128)}, f32[640,640]{1,0:T(8,128)}, f32[640,640]{1,0:T(8,128)})) %all-reduce.15.cloned.1.call-update) | async-done | bytes 4915216 | tf_op jit(solution)/shard_map/psum | solution.py:220
  956.6 1.4 copy.129
  958.0 2.8 copy.130
  (124 shorter events, 32.6 us)
Async XLA Ops:
  7.2 61.2 %copy-start = (bf16[640,640]{1,0:T(8,128)(2,1)S(1)}, bf16[640,640]{1,0:T(8,128)(2,1)}, u32[]{:S(2)}) copy-start(bf16[640,640]{1,0:T(8,128)(2,1)} %param.20) | copy-start | bytes 2457604
  7.2 114.7 %all-reduce.9.cloned.1.call-start = ((), (), s32[]{:S(2)}) async-start(), calls=%async_computation.2 | async-start | bytes 2621440
  59.6 5.0 copy-start.16
  59.8 5.6 copy-start.11
  65.4 1.1 copy-start.1
  66.5 1.9 copy-start.10
  71.0 0.7 copy-start.19
  71.0 2.0 copy-start.14
  71.0 322.6 %all-reduce.11.cloned.1.call-start = ((), (), s32[]{:S(2)}) async-start(), calls=%async_computation.3 | async-start | bytes 2359296
  71.5 1.7 copy-start.9
  122.9 1.0 copy-start.3
  122.9 1.1 copy-start.18
  129.2 2.3 copy-start.17
  130.6 375.0 %reduce-scatter.3.cloned.1.call-start = ((), (), s32[]{:S(2)}) async-start(), calls=%async_computation.1 | async-start | bytes 819200 | tf_op jit(solution)/shard_map/reduce_scatter | solution.py:201
  473.0 2.9 copy-start.2
  475.8 0.9 copy-start.4
  475.9 1.1 copy-start.6
  475.9 1.6 copy-start.12
  483.8 273.5 %all-reduce.13.cloned.1.call-start = ((), (), s32[]{:S(2)}) async-start(), calls=%async_computation.4 | async-start | bytes 163840 | tf_op jit(solution)/shard_map/psum | solution.py:219
  501.0 7.9 copy-start.5
  508.9 447.7 %all-reduce.15.cloned.1.call-start = ((), (), s32[]{:S(2)}) async-start(), calls=%async_computation.5 | async-start | bytes 9830400 | tf_op jit(solution)/shard_map/psum | solution.py:220
  511.0 0.9 copy-start.13
  958.0 2.8 copy-start.8
  960.9 2.0 copy-start.7
  962.9 1.2 copy-start.15
Sparse Core Ops, SparseCore 0:
  71.1 50.6 all-reduce.8
  130.7 262.8 all-reduce.10
  483.9 21.6 reduce-scatter.2
  511.7 245.4 all-reduce.12
  761.6 195.0 all-reduce.14
where the time goes:
time: 972 us; the launch traced here: 971 us
  waiting for transfers between devices  748 us (77%)
  blocking collectives  131 us (13%)
  local copies, waits for them, and re-layouts  45.9 us (5%)
  matrix products  22.9 us (2%)
  between operations  14.9 us (2%)
    unnamed x7, waiting for transfers between devices  309 us
    psum x1, waiting for transfers between devices, per_device(): grad_in, grad_out = lax.psum((in_term, out_term), ('tile', 'mp'))  236 us
    psum x1, waiting for transfers between devices, per_device(): lax.psum((value_term, gate_term, down_term), 'tile')  199 us
    all_gather x1, blocking collectives, per_device(): cot_source = lax.all_gather(share_cot, ('tile', 'mp'), axis=0, tiled=True)  70.2 us
    all_gather x1, blocking collectives, per_device(): latent_source = lax.all_gather(latent, 'tile', axis=0, tiled=True)  51.5 us
  transfers between devices with their start and end apart: 5, of which 5 were waited for; matrix products, arithmetic and copies ran while one was open for 3% of the time, Pallas kernels for 0%

commit v1 on v0

--- a/solution.py
+++ b/solution.py
@@ -9,6 +9,13 @@
 root_half = 0.7071067811865476
 inv_root_two_pi = 0.3989422804014327
 highest = lax.Precision.HIGHEST
+
+
+def exchange_gather(x, axis, dim):
+    peers = lax.axis_size(axis)
+    blocks = jnp.stack([x for _ in range(peers)])
+    blocks = lax.all_to_all(blocks, axis, split_axis=0, concat_axis=0)
+    return jnp.concatenate(blocks, axis=dim)
 
 
 def gelu_value(inputs):
@@ -176,7 +183,7 @@
         jnp.bfloat16
     )
     blended = lax.all_gather(share_blend, "mp", axis=0, tiled=True)
-    cot_source = lax.all_gather(share_cot, ("tile", "mp"), axis=0, tiled=True)
+    cot_source = exchange_gather(share_cot, ("tile", "mp"), 0)
     cot_patches = crop_tiles(cot_source, offsets, tile_side, channels)
     cot_flat = jnp.transpose(cot_patches, (1, 0, 2)).reshape(token_count * tiles_here, 4 * channels)
     cot_share = take_share(cot_flat)

time: 972 us -> 934 us (0.961)
  blocking collectives: 131 us -> 60.6 us
  waiting for transfers between devices: 748 us -> 770 us
    all_gather x1 -> x0, blocking collectives: 70.2 us -> none  [per_device(): cot_source = lax.all_gather(share_cot, ('tile', 'mp'), axis=0, tiled=True)]
    all_to_all x0 -> x1, waiting for transfers between devices: none -> 20.8 us  [exchange_gather(): blocks = lax.all_to_all(blocks, axis, split_axis=0, concat_axis=0)]
  transfers between devices with their start and end apart: 5 -> 6, of which waited for: 5 -> 6; matrix products, arithmetic and copies ran while one was open for 3% -> 3% of each run, Pallas kernels for 0% -> 0%
where the time goes in v1:
time: 934 us; the launch traced here: 933 us
  waiting for transfers between devices  770 us (82%)
  blocking collectives  60.6 us (6%)
  local copies, waits for them, and re-layouts  47 us (5%)
  matrix products  22.9 us (2%)
  between operations  14.8 us (2%)
  starting transfers between devices  9.73 us (1%)
    unnamed x7, waiting for transfers between devices  312 us
    psum x1, waiting for transfers between devices, per_device(): grad_in, grad_out = lax.psum((in_term, out_term), ('tile', 'mp'))  236 us
    psum x1, waiting for transfers between devices, per_device(): lax.psum((value_term, gate_term, down_term), 'tile')  199 us
    all_gather x1, blocking collectives, per_device(): latent_source = lax.all_gather(latent, 'tile', axis=0, tiled=True)  51.5 us
    all_to_all x1, waiting for transfers between devices, exchange_gather(): blocks = lax.all_to_all(blocks, axis, split_axis=0, concat_axis=0)  20.8 us
  transfers between devices with their start and end apart: 6, of which 6 were waited for; matrix products, arithmetic and copies ran while one was open for 3% of the time, Pallas kernels for 0%

profile of v1, /device:TPU:97, one launch (start us, length us, event | category | flops | bytes accessed | tf_op | source)
XLA Modules:
  0.0 932.6 jit_solution(6358419212517309448)
XLA Ops:
  8.1 51.5 %all-gather = bf16[64,12,384]{2,1,0:T(8,128)(2,1)S(1)} all-gather(bf16[1,12,384]{2,1,0:T(8,128)(2,1)} %bitcast.105), channel_id=1, replica_groups=mesh['tile'=64,'mp'=4] {'tile'}, dimensions={0}, use_global_device_ids=true | all-gather | bytes 599040 | tf_op jit(solution)/shard_map/all_gather | solution.py:129
  59.8 4.0 while.16
  60.4 1.4 bitcast_dynamic-update-slice_fusion.4
  66.5 1.9 multiply_convert_fusion.1
  69.2 1.8 reshape.148
  73.1 48.8 %all-reduce.9.cloned.1.call-done = f32[256,2,640]{2,1,0:T(2,128)} async-done(((f32[256,2,640]{2,1,0:T(2,128)}), f32[256,2,640]{2,1,0:T(2,128)}) %all-reduce.9.cloned.1.call-update) | async-done | bytes 1310736
  124.1 5.1 while.15
  130.9 262.6 %all-reduce.11.cloned.1.call-done = f32[768,384]{0,1:T(8,128)} async-done(((f32[768,384]{0,1:T(8,128)}), f32[768,384]{0,1:T(8,128)}) %all-reduce.11.cloned.1.call-update) | async-done | bytes 1179664
  397.3 9.3 %all-to-all-start = ((bf16[256,3,384]{2,1,0:T(4,128)(2,1)}), bf16[256,3,384]{2,1,0:T(4,128)(2,1)S(1)}, u32[]{:S(2)}, u32[]{:S(2)}) async-start(bf16[256,3,384]{2,1,0:T(4,128)(2,1)} %stack.2), calls=%async_computation | async-start | bytes 1572864 | tf_op jit(solution)/shard_map/all_to_all | solution.py:17
  408.9 20.8 %all-to-all-done = bf16[256,3,384]{2,1,0:T(4,128)(2,1)S(1)} async-done(((bf16[256,3,384]{2,1,0:T(4,128)(2,1)}), bf16[256,3,384]{2,1,0:T(4,128)(2,1)S(1)}, u32[]{:S(2)}, u32[]{:S(2)}) %all-to-all-start) | async-done | bytes 589856 | tf_op jit(solution)/shard_map/all_to_all | solution.py:17
  430.3 4.0 while.17
  430.9 1.4 bitcast_dynamic-update-slice_fusion.5
  432.9 1.4 bitcast_dynamic-update-slice_fusion.5
  437.0 2.9 fusion.9
  441.5 1.6 fusion.2
  443.1 2.6 convert_element_type.57
  445.7 2.0 copy.98
  448.7 2.9 reshape.158
  451.6 1.8 constant_dynamic-slice_fusion.3
  453.4 1.8 reshape.157
  455.2 1.8 constant_dynamic-slice_fusion.5
  458.3 1.8 fusion.10
  460.1 3.1 fusion.33
  463.2 1.9 fusion.17
  465.1 2.1 reduce-scatter.3.cloned.1.call-done
  468.4 2.1 convolution_bitcast_fusion.2
  470.5 2.0 fusion.35
  473.3 9.1 all-gather.1
  483.0 235.7 %all-reduce.13.cloned.1.call-done = (f32[16,640]{1,0:T(8,128)}, f32[640,16]{0,1:T(8,128)}) async-done(((f32[16,640]{1,0:T(8,128)}, f32[640,16]{0,1:T(8,128)}), (f32[16,640]{1,0:T(8,128)}, f32[640,16]{0,1:T(8,128)})) %all-reduce.13.cloned.1.call-update) | async-done | bytes 81936 | tf_op jit(solution)/shard_map/psum | solution.py:226
  718.7 199.4 %all-reduce.15.cloned.1.call-done = (f32[640,640]{1,0:T(8,128)}, f32[640,640]{1,0:T(8,128)}, f32[640,640]{1,0:T(8,128)}) async-done(((f32[640,640]{1,0:T(8,128)}, f32[640,640]{1,0:T(8,128)}, f32[640,640]{1,0:T(8,128)}), (f32[640,640]{1,0:T(8,128)}, f32[640,640]{1,0:T(8,128)}, f32[640,640]{1,0:T(8,128)})) %all-reduce.15.cloned.1.call-update) | async-done | bytes 4915216 | tf_op jit(solution)/shard_map/psum | solution.py:227
  918.0 1.4 copy.146
  919.4 2.8 copy.147
  (124 shorter events, 35.1 us)
Async XLA Ops:
  7.2 61.2 %copy-start = (bf16[640,640]{1,0:T(8,128)(2,1)S(1)}, bf16[640,640]{1,0:T(8,128)(2,1)}, u32[]{:S(2)}) copy-start(bf16[640,640]{1,0:T(8,128)(2,1)} %param.20) | copy-start | bytes 2457604
  7.2 114.7 %all-reduce.9.cloned.1.call-start = ((), (), s32[]{:S(2)}) async-start(), calls=%async_computation.3 | async-start | bytes 2621440
  59.6 5.0 copy-start.16
  59.8 5.6 copy-start.11
  65.4 1.1 copy-start.1
  66.5 1.9 copy-start.10
  71.0 0.7 copy-start.19
  71.0 1.9 copy-start.13
  71.0 322.5 %all-reduce.11.cloned.1.call-start = ((), (), s32[]{:S(2)}) async-start(), calls=%async_computation.4 | async-start | bytes 2359296
  71.5 1.6 copy-start.9
  122.9 1.0 copy-start.3
  122.9 1.1 copy-start.18
  129.1 1.4 copy-start.17
  397.3 32.5 %all-to-all-start = ((bf16[256,3,384]{2,1,0:T(4,128)(2,1)}), bf16[256,3,384]{2,1,0:T(4,128)(2,1)S(1)}, u32[]{:S(2)}, u32[]{:S(2)}) async-start(bf16[256,3,384]{2,1,0:T(4,128)(2,1)} %stack.2), calls=%async_computation | async-start | bytes 1572864 | tf_op jit(solution)/shard_map/all_to_all | solution.py:17
  406.6 60.6 %reduce-scatter.3.cloned.1.call-start = ((), (), s32[]{:S(2)}) async-start(), calls=%async_computation.2 | async-start | bytes 819200 | tf_op jit(solution)/shard_map/reduce_scatter | solution.py:208
  437.0 2.9 copy-start.2
  439.8 0.8 copy-start.4
  439.8 1.1 copy-start.6
  439.9 1.6 copy-start.12
  447.8 270.9 %all-reduce.13.cloned.1.call-start = ((), (), s32[]{:S(2)}) async-start(), calls=%async_computation.5 | async-start | bytes 163840 | tf_op jit(solution)/shard_map/psum | solution.py:226
  465.1 5.4 copy-start.5
  470.5 447.6 %all-reduce.15.cloned.1.call-start = ((), (), s32[]{:S(2)}) async-start(), calls=%async_computation.6 | async-start | bytes 9830400 | tf_op jit(solution)/shard_map/psum | solution.py:227
  472.6 0.7 copy-start.15
  919.4 2.8 copy-start.8
  922.3 2.0 copy-start.7
  924.3 1.2 copy-start.14
Sparse Core Ops, SparseCore 0:
  71.1 50.6 all-reduce.8
  130.7 262.8 all-reduce.10
  447.9 19.2 reduce-scatter.2
  473.3 245.3 all-reduce.12
  723.0 195.0 all-reduce.14
